TPU v7x, 128 devices: a whole 4x4x4 slice. The times are simulated.
128 devices in a mesh: seq: 32 (over x, y, core), ch: 4 (over z).
Axes of the slice: x: 4, y: 4, z: 4, core: 2. Of those that a mesh axis runs over, the one named last changes fastest.
Arguments:
- query_feat: bfloat16 [32768, 4096], P('seq', 'ch'), may hold values from -6 to 6
- key_feat: bfloat16 [32768, 4096], P('seq', 'ch'), may hold values from -6 to 6
- value_feat: bfloat16 [32768, 4096], P('seq', 'ch'), may hold values from -6 to 6
- decay_rates: float32 [256, 16], P('ch'), may hold values from 6.1035156e-06 to 0.041666667
- residues: float32 [256, 16], P('ch'), may hold values from -0.28867513 to 0.28867513
- out_weight: bfloat16 [4096, 4096], P('ch', 'seq'), may hold values from -0.09375 to 0.09375
Outputs:
- mixed: bfloat16 [32768, 4096], P(('seq', 'ch'))
All inputs are finite; a program needn't handle non-finite values.
Results may differ from a plain program's by a relative error of at most 0.014.
Values may be sent and summed in bfloat16 or wider, within the bound.
A program may use at most 128 MiB of HBM per device.

v0:
```python
import jax
import jax.numpy as jnp
from jax import lax
from jax.sharding import PartitionSpec as P

SUB = 256


def band_matrix(filter_taps, block):
    group_count = filter_taps.shape[0]
    flipped = jnp.concatenate(
        [jnp.flip(filter_taps, axis=1), jnp.zeros((group_count, block), filter_taps.dtype)], axis=1
    )
    tiled = jnp.tile(flipped, (1, block))[:, : block * (2 * block - 1)]
    return tiled.reshape(group_count, block, 2 * block - 1)[:, :, block - 1 :]


def on_device(query_feat, key_feat, value_feat, decay_rates, residues, out_weight):
    tok_rows, width_dev = query_feat.shape
    group_count, mode_count = decay_rates.shape
    group_width = width_dev // group_count
    block_count = tok_rows // SUB
    hi = lax.Precision.HIGHEST
    mixed_u = (key_feat.astype(jnp.float32) * value_feat.astype(jnp.float32)).astype(jnp.bfloat16)
    lag_steps = jnp.arange(SUB, dtype=jnp.float32)
    filter_taps = jnp.sum(
        residues[:, :, None] * jnp.exp(-decay_rates[:, :, None] * lag_steps), axis=1
    ).astype(jnp.bfloat16)
    toeplitz = band_matrix(filter_taps, SUB)
    inject = jnp.exp(-decay_rates[:, :, None] * (SUB - 1.0 - lag_steps)).astype(jnp.bfloat16)
    readout = residues[:, :, None] * jnp.exp(-decay_rates[:, :, None] * (lag_steps + 1.0))
    rates_mode = decay_rates.T[:, :, None]
    step_decay = jnp.exp(-rates_mode * SUB)
    blocks_u = mixed_u.reshape(block_count, SUB, group_count, group_width)
    local_part = jnp.einsum(
        "gab,nbgc->nagc", toeplitz, blocks_u, preferred_element_type=jnp.float32
    )
    block_sums = jnp.einsum("gmb,nbgc->nmgc", inject, blocks_u, preferred_element_type=jnp.float32)
    prefix = [jnp.zeros((mode_count, group_count, group_width), jnp.float32)]
    for block in range(block_count):
        prefix.append(step_decay * prefix[-1] + block_sums[block])
    final_state = prefix[block_count]
    starts = jnp.stack(prefix[:block_count])
    my_index = lax.axis_index("seq")
    piece = lax.all_gather(
        final_state[None].astype(jnp.bfloat16), "seq", axis=0, tiled=True
    ).astype(jnp.float32)
    positions = jnp.arange(piece.shape[0], dtype=jnp.int32)
    lag_count = my_index - 1 - positions
    live = lag_count >= 0
    lag_float = jnp.maximum(lag_count, 0).astype(jnp.float32) * tok_rows
    weights = jnp.exp(-rates_mode[None] * lag_float[:, None, None, None])
    weights = jnp.where(live[:, None, None, None], weights, 0.0)
    incoming = jnp.zeros_like(final_state) + jnp.sum(weights * piece, axis=0)
    offsets = (SUB * jnp.arange(block_count, dtype=jnp.float32))[:, None, None, None]
    entering = starts + jnp.exp(-rates_mode[None] * offsets) * incoming[None]
    carried = jnp.einsum("gma,nmgc->nagc", readout, entering, precision=hi)
    gate_q = query_feat.reshape(block_count, SUB, group_count, group_width).astype(jnp.float32)
    gated = (gate_q * (local_part + carried)).astype(jnp.bfloat16).reshape(tok_rows, width_dev)
    weight_cols = lax.all_gather(out_weight, "seq", axis=1, tiled=True)
    return lax.psum_scatter(
        jnp.dot(gated, weight_cols, preferred_element_type=jnp.float32).astype(jnp.bfloat16),
        "ch",
        scatter_dimension=0,
        tiled=True,
    )


def solution(mesh):
    in_specs = (
        P("seq", "ch"),
        P("seq", "ch"),
        P("seq", "ch"),
        P("ch", None),
        P("ch", None),
        P("ch", "seq"),
    )
    out_specs = P(("seq", "ch"), None)
    return jax.shard_map(
        on_device, mesh=mesh, in_specs=in_specs, out_specs=out_specs, check_vma=False
    )
```

profile of v0, /device:TPU:1, one launch (start us, length us, event | category | flops | bytes accessed | tf_op | source)
XLA Modules:
  0.0 244.9 jit_solution(16450819888071427563)
XLA Ops:
  6.5 0.7 negate_bitcast_fusion
  7.2 0.7 broadcast_multiply_fusion
  7.9 0.1 copy.73
  8.0 3.2 %multiply_convert_fusion = bf16[1024,1024]{1,0:T(8,128)(2,1)S(1)} fusion(bf16[1024,1024]{1,0:T(8,128)(2,1)} %param.8, bf16[1024,1024]{1,0:T(8,128)(2,1)} %param.7), kind=kLoop, calls=%fused_computation.6 | loop fusion | flops 4194304 | bytes 6291456 | tf_op jit(solution)/shard_map/convert_element_type | solution.py:24
  11.2 2.6 %copy.71 = bf16[1024,1024]{0,1:T(8,128)(2,1)} copy(bf16[1024,1024]{1,0:T(8,128)(2,1)S(1)} %multiply_convert_fusion) | data formatting | bytes 4194304 | tf_op jit(solution)/shard_map/convert_element_type | solution.py:24
  13.8 3.3 %reshape.69 = bf16[4,256,64,16]{1,0,3,2:T(4,128)(2,1)S(1)} reshape(bf16[1024,1024]{0,1:T(8,128)(2,1)} %copy.71) | data formatting | bytes 4194304 | tf_op jit(solution)/shard_map/reshape | solution.py:34
  17.1 2.1 fusion.2
  19.2 2.8 %copy.76 = f32[64,4,16,16]{0,2,3,1:T(8,128)S(1)} copy(f32[64,4,16,16]{3,2,1,0:T(8,128)} %fusion.2) | data formatting | bytes 524288 | tf_op jit(solution)/shard_map/gmb,nbgc->nmgc/dot_general | solution.py:38
  22.0 0.7 fusion.16
  22.7 0.0 all-gather.5.cloned.1.call-start
  22.7 0.7 all-gather.5.cloned.1.call-update
  23.5 0.2 reduce-scatter.2.cloned.1.call-start
  23.7 0.1 copy.72
  23.8 0.4 multiply_reduce_fusion.1
  24.2 0.2 rev.4
  24.4 1.4 tile.4
  25.8 38.5 %copy.86 = bf16[8,8,256,512]{3,1,2,0:T(8,128)(2,1)S(1)} copy(bf16[8,8,256,512]{3,2,1,0:T(8,128)(2,1)S(1)} %bitcast.40) | data formatting | bytes 33554432
  64.4 6.5 %slice.24 = bf16[64,130816]{1,0:T(8,128)(2,1)} slice(bf16[64,131072]{1,0:T(8,128)(2,1)S(1)} %bitcast.41), slice={[0:64], [0:130816]} | slice | bytes 33488896 | tf_op jit(solution)/shard_map/slice | solution.py:14
  70.9 36.0 %reshape.70 = bf16[64,256,511]{2,1,0:T(8,128)(2,1)} reshape(bf16[64,130816]{1,0:T(8,128)(2,1)} %slice.24) | data formatting | bytes 33488896 | tf_op jit(solution)/shard_map/reshape | solution.py:15
  106.9 4.1 %copy.70 = f32[1024,1024]{0,1:T(8,128)} copy(bf16[1024,1024]{1,0:T(8,128)(2,1)} %param.6) | data formatting | bytes 6291456 | tf_op jit(solution)/shard_map/convert_element_type | solution.py:58
  111.1 5.6 %reshape.72 = f32[4,256,64,16]{1,0,3,2:T(4,128)} reshape(f32[1024,1024]{0,1:T(8,128)} %copy.70) | data formatting | bytes 8388608 | tf_op jit(solution)/shard_map/convert_element_type | solution.py:58
  116.8 0.1 multiply_exponential_fusion
  116.8 0.1 exponential_select_fusion
  117.0 10.0 %fusion = f32[64,4,16,256]{3,2,1,0:T(8,128)} fusion(bf16[64,256,511]{2,1,0:T(8,128)(2,1)} %reshape.70, bf16[4,256,64,16]{1,0,3,2:T(4,128)(2,1)S(1)} %reshape.69), kind=kOutput, calls=%fused_computation.1 | convolution fusion | flops 536870912 | bytes 14680064 | tf_op jit(solution)/shard_map/gab,nbgc->nagc/dot_general | solution.py:35
  126.9 2.2 multiply_reduce_fusion
  129.1 0.1 maximum_add_fusion
  129.2 1.9 copy.79
  131.1 7.3 %fusion.1 = bf16[4,256,64,16]{1,3,0,2:T(8,128)(2,1)S(1)} fusion(f32[4,256,64,16]{1,0,3,2:T(4,128)} %reshape.72, f32[64,4,16,256]{3,2,1,0:T(8,128)} %fusion, f32[4,16,64,16]{1,3,0,2:T(8,128)S(1)} %copy.79, f32[256]{0:T(256)S(1)} %iota_add_fusion, f32[64,16]{1,0:T(8,128)S(1)} %copy.73, f32[64,16]{1,0:T(8,128)S(1)} %copy.72), kind=kOutput, calls=%fused_computation.4 | convolution fusion | flops 204996608 | bytes 10757120 | tf_op jit(solution)/shard_map/gma,nmgc->nagc/dot_general | solution.py:57
  138.4 1.1 copy.81
  139.5 0.5 copy.87
  140.0 14.6 %convolution_convert_fusion = bf16[1024,4096]{1,0:T(8,128)(2,1)} fusion(bf16[1024,1024]{0,1:T(8,128)(2,1)S(1)} %bitcast.44, bf16[1024,4096]{1,0:T(8,128)(2,1)} %all-gather.5.cloned.1.call-done), kind=kOutput, calls=%fused_computation.2 | convolution fusion | flops 8594128896 | bytes 18874368 | tf_op jit(solution)/shard_map/dot_general | solution.py:62
  154.6 83.7 %reduce-scatter.2.cloned.1.call-done = bf16[256,4096]{1,0:T(8,128)(2,1)} async-done(((bf16[1024,4096]{1,0:T(8,128)(2,1)}), bf16[256,4096]{1,0:T(8,128)(2,1)}) %reduce-scatter.2.cloned.1.call-update) | async-done | bytes 2097168 | tf_op jit(solution)/shard_map/reduce_scatter | solution.py:61
  (14 shorter events, 0.1 us)
Async XLA Ops:
  6.5 120.4 %all-gather.3.cloned.1.call-start = ((), (), s32[]{:S(2)}) async-start(), calls=%async_computation.1 | async-start | bytes 2162688 | tf_op jit(solution)/shard_map/all_gather | solution.py:45
  19.2 4.5 %copy-start = (f32[64,16]{0,1:T(8,128)S(1)}, f32[64,16]{0,1:T(8,128)}, u32[]{:S(2)}) copy-start(f32[64,16]{0,1:T(8,128)} %param.10) | copy-start | bytes 12292
  22.7 117.3 %all-gather.5.cloned.1.call-start = ((), (), s32[]{:S(2)}) async-start(), calls=%async_computation.2 | async-start | bytes 8650752 | tf_op jit(solution)/shard_map/all_gather | solution.py:60
  23.5 214.9 %reduce-scatter.2.cloned.1.call-start = ((), (), s32[]{:S(2)}) async-start(), calls=%async_computation.3 | async-start | bytes 10485760 | tf_op jit(solution)/shard_map/reduce_scatter | solution.py:61
Sparse Core Ops, SparseCore 0:
  22.8 47.0 all-gather.2
  72.1 58.0 all-gather.4
  154.7 83.5 reduce-scatter.1
where the time goes:
time: 245 us
  local copies, waits for them, and re-layouts  105 us (43%)
  waiting for transfers between devices  84.5 us (34%)
  matrix products  33.9 us (14%)
  between operations  13.2 us (5%)
  other arithmetic  8.24 us (3%)
    reduce_scatter x1, waiting for transfers between devices, on_device(): lax.psum_scatter(jnp.dot(gated, weight_cols, preferred_element_type=jnp.f...  83.7 us
    unnamed x5, local copies, waits for them, and re-layouts  39.1 us
    reshape x1, local copies, waits for them, and re-layouts, band_matrix(): return tiled.reshape(group_count, block, 2 * block - 1)[:, :, block - 1:]  36 us
    dot_general x1, matrix products, on_device(): jnp.dot(gated, weight_cols, preferred_element_type=jnp.float32)  14.6 us
    dot_general x1, matrix products, on_device(): jnp.einsum('gab,nbgc->nagc', toeplitz, blocks_u, preferred_element_type=j...  9.96 us
    convert_element_type x2, local copies, waits for them, and re-layouts, on_device(): query_feat.reshape(block_count, SUB, group_count, group_width)  9.78 us
    dot_general x1, matrix products, on_device(): carried = jnp.einsum('gma,nmgc->nagc', readout, entering, precision=hi)  7.31 us
    slice x1, local copies, waits for them, and re-layouts, band_matrix(): tiled = jnp.tile(flipped, (1, block))[:, :block * (2 * block - 1)]  6.51 us
  transfers between devices with their start and end apart: 3, of which 1 were waited for; matrix products, arithmetic and copies ran while one was open for 47% of the time, Pallas kernels for 0%

commit v1 on v0

v1 whole, which is shorter than its diff:
```python
import functools

import jax
import jax.numpy as jnp
from jax import lax
from jax.experimental import pallas as pl
from jax.experimental.pallas import tpu as pltpu
from jax.sharding import PartitionSpec as P

SUB = 256
LANES = 128
TILES = 8
RING = 4
CHIPS = RING * RING
CHUNKS = CHIPS // 2
F32 = jnp.float32
BF16 = jnp.bfloat16
MESH = pl.DeviceIdType.MESH

ORDER = [
    (0, 0), (1, 0), (3, 0), (0, 1), (0, 3), (2, 0), (0, 2), (1, 1),
    (1, 3), (3, 1), (3, 3), (2, 1), (2, 3), (1, 2), (3, 2), (2, 2),
]


def kernel(
    q_hbm, k_hbm, v_hbm, w_hbm, rates_ref, lam_ref, res_ref, taps_ref, out_hbm,
    qb, kb, vb, ub, zloc, band, bs, ent, wb, lhs, send_a, send_b, recv_b, acc, stage,
    st_send, st_sib, st_y, st_x,
    load_sem, sib_sem, st_sem, w_send, w_recv, a_sem, b_sem, fwd_sem, o_sem,
):
    s = lax.axis_index("seq")
    z = lax.axis_index("ch")
    x = lax.div(s, 8)
    y = lax.rem(lax.div(s, 2), 4)
    c = lax.rem(s, 2)
    par = lax.rem(z, 2)
    z_a = z + 1 - 2 * par
    z_b = 3 - z
    sib = s + 1 - 2 * c

    def at_xy(dx, dy):
        return (lax.rem(x + dx, 4) * 4 + lax.rem(y + dy, 4)) * 2 + c

    def chip(dx, dy):
        return lax.rem(x + dx, 4) * 4 + lax.rem(y + dy, 4)

    pending = []

    def remote(src, dst, ssem, rsem, dev):
        return pltpu.make_async_remote_copy(
            src_ref=src, dst_ref=dst, send_sem=ssem, recv_sem=rsem, device_id=dev, device_id_type=MESH
        )

    def send(src, dst, ssem, rsem, dev):
        cp = remote(src, dst, ssem, rsem, dev)
        cp.start()
        pending.append(cp)

    loads = []
    for i, (src, dst) in enumerate(((k_hbm, kb), (v_hbm, vb), (q_hbm, qb))):
        loads.append(pltpu.make_async_copy(src, dst, load_sem.at[i]))
    for r in range(2):
        loads.append(
            pltpu.make_async_copy(w_hbm.at[pl.ds(r * 512, 512), :], wb.at[chip(0, 0), r, par], load_sem.at[3 + r])
        )
    for cp in loads:
        cp.start()

    partners = [(sib, z), (s, z_a), (s, z_b)]
    partners += [(at_xy(d, 0), z) for d in (1, 2, 3)] + [(at_xy(0, d), z) for d in (1, 2, 3)]
    barrier = pltpu.get_barrier_semaphore()
    for dev in partners:
        pl.semaphore_signal(barrier, inc=1, device_id=dev, device_id_type=MESH)
    pl.semaphore_wait(barrier, len(partners))

    own = chip(0, 0)
    for r in range(2):
        send(w_hbm.at[pl.ds(r * 512, 512), :], wb.at[own, r, par], w_send.at[r], w_recv.at[r], (s, z_a))

    send_slots = {}
    recv_slots = {}

    def slot_of(table, base, key):
        if key not in table:
            table[key] = base + len(table)
        return table[key]

    def to_xy(r, df, dg):
        return (df, dg) if r == 0 else (dg, df)

    def w_copy(r, origin, step, half, key):
        slot = chip(*to_xy(r, *origin))
        ref = wb.at[slot, r] if half is None else wb.at[slot, r, half]
        ss = slot_of(send_slots, 2, (r, origin, step, half))
        rs = slot_of(recv_slots, 2, (r,) + key)
        return remote(ref, ref, w_send.at[ss], w_recv.at[rs], (at_xy(*to_xy(r, *step)), z))

    def w_hop(r, origin, step, half):
        key = ((origin[0] - step[0]) % 4, (origin[1] - step[1]) % 4, half)
        cp = w_copy(r, origin, step, half, key)
        cp.start()
        pending.append(cp)

    def w_wait(r, rel, half):
        slot = chip(*to_xy(r, *rel))
        ref = wb.at[slot, r] if half is None else wb.at[slot, r, half]
        rs = slot_of(recv_slots, 2, (r, rel[0], rel[1], half))
        remote(ref, ref, w_send.at[0], w_recv.at[rs], (s, z)).wait_recv()

    arrived = set()

    def arrive(r, rel):
        if (r, rel) in arrived:
            return
        arrived.add((r, rel))
        df, dg = rel
        if rel == (0, 0):
            w_hop(r, rel, (1, 0), None)
            w_hop(r, rel, (3, 0), None)
            w_hop(r, rel, (0, 1), None)
            w_hop(r, rel, (0, 3), None)
            return
        on_f = dg == 0
        d = df if on_f else dg
        if d == 2:
            w_wait(r, rel, 0)
            w_wait(r, rel, 1)
        else:
            w_wait(r, rel, None)
            fwd = 1 if d == 3 else 3
            w_hop(r, rel, (fwd, 0) if on_f else (0, fwd), 0 if d == 3 else 1)
        if on_f:
            w_hop(r, rel, (0, 1), None)
            w_hop(r, rel, (0, 3), None)

    def weights_start():
        for r in range(2):
            loads[3 + r].wait()
            slab = wb.at[own, r, 1 - par]
            remote(slab, slab, w_send.at[0], w_recv.at[r], (s, z_a)).wait_recv()
        for r in range(2):
            arrive(r, (0, 0))

    loads[0].wait()
    loads[1].wait()
    lane_group = lax.div(lax.rem(lax.broadcasted_iota(jnp.int32, (1, 2 * LANES), 1), LANES), 16)

    def sums_tile(t, carry):
        lanes = pl.ds(pl.multiple_of(t * LANES, LANES), LANES)
        u = (kb[:, lanes].astype(F32) * vb[:, lanes].astype(F32)).astype(BF16)
        ub[:, lanes] = u
        lam = lam_ref[0:1, lanes]
        back = 255.0 - lax.broadcasted_iota(jnp.int32, (SUB, LANES), 0).astype(F32)
        inject = jnp.exp(-lam * back).T.astype(BF16)
        for p in range(2):
            rhs = jnp.concatenate([u[512 * p : 512 * p + 256], u[512 * p + 256 : 512 * p + 512]], axis=1)
            full = jnp.dot(inject, rhs, preferred_element_type=F32)
            total = jnp.zeros((16, 2 * LANES), F32)
            for g in range(8):
                total = jnp.where(lane_group == g, full[16 * g : 16 * g + 16], total)
            bs[2 * p, :, lanes] = total[:, :LANES]
            bs[2 * p + 1, :, lanes] = total[:, LANES:]
        return carry

    lax.fori_loop(0, TILES, sums_tile, 0)

    def decay(steps):
        return jnp.exp(rates_ref[...] * (-steps))

    block_decay = decay(256.0)
    ent[1] = bs[0]
    ent[2] = block_decay * ent[1] + bs[1]
    ent[3] = block_decay * ent[2] + bs[2]
    final = block_decay * ent[3] + bs[3]
    ent[0] = final
    st_send[0] = final.astype(BF16)
    send(st_send.at[0], st_sib, st_sem.at[0, 0], st_sem.at[1, 0], (sib, z))

    weights_start()

    row_i = lax.broadcasted_iota(jnp.int32, (LANES, SUB), 0)
    col_i = lax.broadcasted_iota(jnp.int32, (LANES, SUB), 1)
    above = col_i - row_i > LANES

    def conv_tile(t, carry):
        lanes = pl.ds(pl.multiple_of(t * LANES, LANES), LANES)
        rows = taps_ref[pl.ds(pl.multiple_of(t * 8, 8), 8), :]
        for g in range(8):
            wide = jnp.broadcast_to(rows[g : g + 1, :], (LANES, SUB))
            low = pltpu.roll(wide, 0, 1, stride=1, stride_axis=0)
            low = jnp.where(above, 0.0, low)
            top = jnp.concatenate([low[:, LANES:], jnp.zeros((LANES, LANES), F32)], axis=1)
            band[pl.ds(g * 256, 128), :] = top.astype(BF16)
            band[pl.ds(g * 256 + 128, 128), :] = low.astype(BF16)
        for p in range(2):
            u0 = ub[pl.ds(512 * p, 256), lanes]
            u1 = ub[pl.ds(512 * p + 256, 256), lanes]
            rhs = jnp.concatenate([u0, u1], axis=1)
            local = jnp.zeros((SUB, 2 * LANES), F32)
            for g in range(8):
                part = jnp.dot(band[pl.ds(g * 256, 256), :], rhs, preferred_element_type=F32)
                local = jnp.where(lane_group == g, part, local)
            zloc[pl.ds(512 * p, 256), lanes] = local[:, :LANES]
            zloc[pl.ds(512 * p + 256, 256), lanes] = local[:, LANES:]
        return carry

    def st_wait(buf, i):
        remote(buf, buf, st_sem.at[0, i], st_sem.at[1, i], (s, z)).wait_recv()

    xf, yf = x.astype(F32), y.astype(F32)

    lax.fori_loop(0, 2, conv_tile, 0)

    st_wait(st_sib, 0)
    mine, other = ent[0], st_sib[...].astype(F32)
    first = jnp.where(c == 0, mine, other)
    second = jnp.where(c == 0, other, mine)
    chip_total = decay(1024.0) * first + second
    ent[0] = first
    st_send[1] = chip_total.astype(BF16)
    for d in (1, 3, 2):
        send(st_send.at[1], st_y.at[d - 1], st_sem.at[0, d], st_sem.at[1, d], (at_xy(0, d), z))
    bs[0] = chip_total

    lax.fori_loop(2, 5, conv_tile, 0)
    for r in range(2):
        arrive(r, (1, 0))
        arrive(r, (3, 0))

    row_total = decay(2048.0 * (3.0 - yf)) * bs[0]
    before = jnp.zeros((16, 1024), F32)
    for d in (1, 2, 3):
        st_wait(st_y.at[d - 1], d)
        got = st_y[d - 1].astype(F32)
        from_y = lax.rem(y + 4 - d, 4).astype(F32)
        row_total = row_total + decay(2048.0 * (3.0 - from_y)) * got
        before = before + jnp.where(y >= d, decay(2048.0 * (d - 1)) * got, 0.0)
    st_send[2] = row_total.astype(BF16)
    for d in (1, 3, 2):
        send(st_send.at[2], st_x.at[d - 1], st_sem.at[0, 3 + d], st_sem.at[1, 3 + d], (at_xy(d, 0), z))
    bs[1] = before

    lax.fori_loop(5, TILES, conv_tile, 0)

    far = jnp.zeros((16, 1024), F32)
    for d in (1, 2, 3):
        st_wait(st_x.at[d - 1], 3 + d)
        far = far + jnp.where(x >= d, decay(8192.0 * (d - 1)) * st_x[d - 1].astype(F32), 0.0)
    earlier = bs[1] + decay(2048.0 * yf) * far
    incoming = jnp.where(c == 0, earlier, decay(1024.0) * earlier + ent[0])
    ent[0] = incoming
    for n in range(1, 4):
        ent[n] = ent[n] + decay(256.0 * n) * incoming

    loads[2].wait()
    diag = lax.div(lax.broadcasted_iota(jnp.int32, (LANES, LANES), 0), 16) == lax.div(
        lax.broadcasted_iota(jnp.int32, (LANES, LANES), 1), 16
    )

    def gate(i, n0, n1):
        def gate_tile(t, carry):
            lanes = pl.ds(pl.multiple_of(t * LANES, LANES), LANES)
            lam = lam_ref[0:1, lanes]
            step = lax.broadcasted_iota(jnp.int32, (SUB, LANES), 0).astype(F32) + 1.0
            read = res_ref[0:1, lanes] * jnp.exp(-lam * step)
            read_hi = read.astype(BF16)
            read_lo = (read - read_hi.astype(F32)).astype(BF16)
            his, los = [], []
            for n in (n0, n1):
                e = ent[n, :, lanes]
                e = jnp.where(diag, jnp.concatenate([e] * 8, axis=0), 0.0)
                hi = e.astype(BF16)
                his.append(hi)
                los.append((e - hi.astype(F32)).astype(BF16))
            hi = jnp.concatenate(his, axis=1)
            lo = jnp.concatenate(los, axis=1)
            carried = jnp.dot(
                jnp.concatenate([read_hi, read_hi, read_lo], axis=1),
                jnp.concatenate([hi, lo, hi], axis=0),
                preferred_element_type=F32,
            )
            for k, (n, dst) in enumerate(((n0, send_a.at[i]), (n1, lhs.at[i, par]))):
                rows = pl.ds(pl.multiple_of(n * 256, 256), 256)
                zz = zloc[rows, lanes] + carried[:, k * LANES : (k + 1) * LANES]
                dst[pl.ds(0, 256), lanes] = (qb[rows, lanes].astype(F32) * zz).astype(BF16)
            return carry

        lax.fori_loop(0, TILES, gate_tile, 0)
        send(send_a.at[i], lhs.at[i, par, pl.ds(0, 256)], a_sem.at[0, i], a_sem.at[1, i], (s, z_a))
        send(
            lhs.at[i, par, pl.ds(0, 256)], lhs.at[i, par, pl.ds(256, 256)],
            fwd_sem.at[0, i, 0], fwd_sem.at[1, i, 0], (sib, z),
        )

    gate(0, 3 - z_a, 3 - z)
    gate(1, z_a, z)

    for r in range(2):
        arrive(r, (2, 0))

    def gathered(i):
        ref = lhs.at[i, 1 - par, pl.ds(0, 256)]
        remote(ref, ref, a_sem.at[0, i], a_sem.at[1, i], (s, z_a)).wait_recv()
        send(
            ref, lhs.at[i, 1 - par, pl.ds(256, 256)],
            fwd_sem.at[0, i, 1], fwd_sem.at[1, i, 1], (sib, z),
        )

    def gathered_sib(i):
        for f, h in ((0, par), (1, 1 - par)):
            ref = lhs.at[i, h, pl.ds(256, 256)]
            remote(ref, ref, fwd_sem.at[0, i, f], fwd_sem.at[1, i, f], (sib, z)).wait_recv()

    def multiply(i, j):
        def half(m, carry):
            rows = pl.ds(pl.multiple_of(m * 256, 256), 256)
            left = jnp.concatenate([lhs[i, 0, rows, :], lhs[i, 1, rows, :]], axis=1)
            right = jnp.concatenate(
                [
                    jnp.concatenate([wb[chip(*rel), r, h] for rel in ORDER[2 * j : 2 * j + 2]], axis=1)
                    for h in range(2)
                    for r in range(2)
                ],
                axis=0,
            )
            val = jnp.dot(left, right, preferred_element_type=F32)
            if i == 0:
                send_b[j, rows, :] = val.astype(BF16)
            else:
                acc[j, rows, :] = val
            return carry

        lax.fori_loop(0, 2, half, 0)

    def need(j):
        for dx, dy in ORDER[2 * j : 2 * j + 2]:
            arrive(0, (dx, dy))
            arrive(1, (dy, dx))

    def partial(j):
        need(j)
        multiply(0, j)
        send(send_b.at[j], recv_b.at[j], b_sem.at[0, j], b_sem.at[1, j], (s, z_b))

    outs = []

    def finish(j):
        remote(recv_b.at[j], recv_b.at[j], b_sem.at[0, j], b_sem.at[1, j], (s, z_b)).wait_recv()
        val = (acc[j] + recv_b[j].astype(F32)).astype(BF16)
        for k in range(2):
            cols = pl.ds(pl.multiple_of(chip(*ORDER[2 * j + k]) * 256 + c * 128, 128), 128)
            part = val[:, k * LANES : (k + 1) * LANES]
            stage[j, k, 0] = part[:256]
            stage[j, k, 1] = part[256:]
            cp = pltpu.make_async_copy(stage.at[j, k, 0], out_hbm.at[:, cols], o_sem.at[0, 2 * j + k])
            cp.start()
            outs.append(cp)
            send(
                stage.at[j, k, 1], out_hbm.at[:, cols],
                o_sem.at[1, 2 * j + k], o_sem.at[2, 2 * j + k], (sib, z),
            )

    gathered(0)
    gathered_sib(0)
    partial(0)
    partial(1)
    partial(2)
    gathered(1)
    gathered_sib(1)
    multiply(1, 0)
    for j in range(3, CHUNKS):
        partial(j)
        multiply(1, j - 2)
        finish(j - 3)
    multiply(1, CHUNKS - 2)
    multiply(1, CHUNKS - 1)
    for j in range(CHUNKS - 3, CHUNKS):
        finish(j)

    for j in range(CHUNKS):
        for k in range(2):
            cols = pl.ds(pl.multiple_of(chip(*ORDER[2 * j + k]) * 256 + (1 - c) * 128, 128), 128)
            remote(
                stage.at[j, k, 1], out_hbm.at[:, cols],
                o_sem.at[1, 2 * j + k], o_sem.at[2, 2 * j + k], (sib, z),
            ).wait_recv()
    for cp in outs:
        cp.wait()
    for cp in pending:
        cp.wait_send()


def on_device(query_feat, key_feat, value_feat, decay_rates, residues, out_weight):
    groups = decay_rates.shape[0]
    lag = jnp.mod(128 - jnp.arange(SUB), SUB).astype(F32)
    taps = jnp.sum(residues[:, :, None] * jnp.exp(-decay_rates[:, :, None] * lag), axis=1)
    taps = taps.astype(BF16).astype(F32)
    rates = jnp.repeat(decay_rates.T, 16, axis=1)
    lam = decay_rates.reshape(1, -1)
    res = residues.reshape(1, -1)
    n_w = 2 + 2 * (2 + 2) * 5
    hbm = pl.BlockSpec(memory_space=pl.ANY)
    vmem = pl.BlockSpec(memory_space=pltpu.VMEM)
    return pl.pallas_call(
        kernel,
        out_shape=jax.ShapeDtypeStruct((256, 4096), BF16),
        in_specs=[hbm] * 4 + [vmem] * 4,
        out_specs=hbm,
        scratch_shapes=[
            pltpu.VMEM((1024, 1024), BF16),
            pltpu.VMEM((1024, 1024), BF16),
            pltpu.VMEM((1024, 1024), BF16),
            pltpu.VMEM((1024, 1024), BF16),
            pltpu.VMEM((1024, 1024), F32),
            pltpu.VMEM((2048, 256), BF16),
            pltpu.VMEM((4, 16, 1024), F32),
            pltpu.VMEM((4, 16, 1024), F32),
            pltpu.VMEM((CHIPS, 2, 2, 512, 128), BF16),
            pltpu.VMEM((2, 2, 512, 1024), BF16),
            pltpu.VMEM((2, 256, 1024), BF16),
            pltpu.VMEM((CHUNKS, 512, 256), BF16),
            pltpu.VMEM((CHUNKS, 512, 256), BF16),
            pltpu.VMEM((CHUNKS, 512, 256), F32),
            pltpu.VMEM((CHUNKS, 2, 2, 256, 128), BF16),
            pltpu.VMEM((3, 16, 1024), BF16),
            pltpu.VMEM((16, 1024), BF16),
            pltpu.VMEM((3, 16, 1024), BF16),
            pltpu.VMEM((3, 16, 1024), BF16),
            pltpu.SemaphoreType.DMA((5,)),
            pltpu.SemaphoreType.DMA((1,)),
            pltpu.SemaphoreType.DMA((2, 7)),
            pltpu.SemaphoreType.DMA((n_w,)),
            pltpu.SemaphoreType.DMA((n_w,)),
            pltpu.SemaphoreType.DMA((2, 2)),
            pltpu.SemaphoreType.DMA((2, CHUNKS)),
            pltpu.SemaphoreType.DMA((2, 2, 2)),
            pltpu.SemaphoreType.DMA((3, 2 * CHUNKS)),
        ],
        compiler_params=pltpu.CompilerParams(
            collective_id=0, has_side_effects=True, vmem_limit_bytes=60 * 1024 * 1024
        ),
    )(query_feat, key_feat, value_feat, out_weight, rates, lam, res, taps)


def solution(mesh):
    in_specs = (
        P("seq", "ch"),
        P("seq", "ch"),
        P("seq", "ch"),
        P("ch", None),
        P("ch", None),
        P("ch", "seq"),
    )
    out_specs = P(("seq", "ch"), None)
    return jax.shard_map(
        on_device, mesh=mesh, in_specs=in_specs, out_specs=out_specs, check_vma=False
    )
```

time: 245 us -> 122 us (0.50)
  Pallas kernels: 0 us -> 112 us
  local copies, waits for them, and re-layouts: 105 us -> 7.92 us
  waiting for transfers between devices: 84.5 us -> 0 us
  matrix products: 33.9 us -> 0 us
  between operations: 13.2 us -> 0.02 us
  other arithmetic: 8.24 us -> 1.77 us
    pallas_call x0 -> x1, Pallas kernels: none -> 112 us  [on_device(): pl.pallas_call(kernel, out_shape=jax.ShapeDtypeStruct((256, 4096), BF16),...]
    reduce_scatter x1 -> x0, waiting for transfers between devices: 83.7 us -> none  [on_device(): lax.psum_scatter(jnp.dot(gated, weight_cols, preferred_element_type=jnp.f...]
    reshape x2 -> x3, local copies, waits for them, and re-layouts: 39.4 us -> 2.26 us  [the longest x1 0.9 us: on_device(): rates = jnp.repeat(decay_rates.T, 16, axis=1)]
    unnamed x5 -> x3, local copies, waits for them, and re-layouts: 39.1 us -> 4.69 us
    dot_general x4 -> x0, matrix products: 33.9 us -> none  [the longest x1 14.6 us: on_device(): jnp.dot(gated, weight_cols, preferred_element_type=jnp.float32)]
    convert_element_type x4 -> x0, local copies, waits for them, and re-layouts: 13.4 us -> none  [the longest x2 9.78 us: on_device(): query_feat.reshape(block_count, SUB, group_count, group_width)]
    slice x1 -> x0, local copies, waits for them, and re-layouts: 6.51 us -> none  [band_matrix(): tiled = jnp.tile(flipped, (1, block))[:, :block * (2 * block - 1)]]
    convert_element_type x2, other arithmetic: 3.87 us -> 0.63 us  [the longest x1 0.62 us: on_device(): taps = taps.astype(BF16).astype(F32)]
  transfers between devices with their start and end apart: 3 -> 0, of which waited for: 1 -> 0; matrix products, arithmetic and copies ran while one was open for 47% -> 0% of each run, Pallas kernels for 0% -> 0%
where the time goes in v1:
time: 122 us; the launch traced here: 121 us
  Pallas kernels  112 us (92%)
  local copies, waits for them, and re-layouts  7.92 us (6%)
  other arithmetic  1.77 us (1%)
    pallas_call x1, Pallas kernels, on_device(): pl.pallas_call(kernel, out_shape=jax.ShapeDtypeStruct((256, 4096), BF16),...  112 us
    unnamed x3, local copies, waits for them, and re-layouts  4.69 us

profile of v1, /device:TPU:1, one launch (start us, length us, event | category | flops | bytes accessed | tf_op | source)
XLA Modules:
  0.0 121.4 jit_solution(15164404065452535801)
XLA Ops:
  0.0 0.7 neg.4
  0.7 0.1 copy.18
  0.8 0.8 copy.16
  1.6 0.4 multiply_reduce_fusion
  2.0 0.7 reshape.30.res_ref
  2.7 0.6 convert_element_type.19.taps_ref
  3.3 0.8 copy.15
  4.1 0.7 reshape.29.lam_ref
  4.8 0.9 broadcast_in_dim.2
  5.7 0.9 reshape.28.rates_ref
  6.6 111.7 %shard_map.64 = bf16[256,4096]{1,0:T(8,128)(2,1)} custom-call(bf16[1024,1024]{1,0:T(8,128)(2,1)} %q_hbm.1, bf16[1024,1024]{1,0:T(8,128)(2,1)} %k_hbm.1, bf16[1024,1024]{1,0:T(8,128)(2,1)} %v_hbm.1, bf16[1024,128]{1,0:T(8,128)(2,1)} %w_hbm.1, f32[16,1024]{1,0:T(8,128)} %reshape.28.rates_ref, f32[1,1024]{1,0:T(1,128)} %reshape.29.lam_ref, ...), custom_call_target="tpu_custom_call" | custom-call | tf_op jit(solution)/shard_map/pallas_call | solution.py:405
  118.3 3.1 %copy.20 = bf16[256,4096]{1,0:T(8,128)(2,1)} copy(bf16[256,4096]{1,0:T(8,128)(2,1)} %shard_map.64) | data formatting | bytes 4194304
  (1 shorter events, 0.0 us)

commit v2 on v1

--- a/solution.py
+++ b/solution.py
@@ -18,15 +18,39 @@
 MESH = pl.DeviceIdType.MESH
 
 ORDER = [
-    (0, 0), (1, 0), (3, 0), (0, 1), (0, 3), (2, 0), (0, 2), (1, 1),
-    (1, 3), (3, 1), (3, 3), (2, 1), (2, 3), (1, 2), (3, 2), (2, 2),
+    (0, 0), (1, 0), (3, 0), (0, 1), (0, 3), (1, 1), (1, 3), (3, 1),
+    (3, 3), (2, 0), (0, 2), (2, 1), (2, 3), (1, 2), (3, 2), (2, 2),
 ]
 
 
+def tables(decay_ref, resid_ref, rates_ref, lam_ref, res_ref, taps_ref):
+    exact = dict(preferred_element_type=F32, precision=lax.Precision.HIGHEST)
+    rate = decay_ref[...]
+    resid = resid_ref[...]
+    groups = rate.shape[0]
+    eye = (
+        lax.broadcasted_iota(jnp.int32, (16, 16), 0) == lax.broadcasted_iota(jnp.int32, (16, 16), 1)
+    ).astype(F32)
+    by_mode = lax.dot_general(eye, rate, (((1,), (1,)), ((), ())), **exact)
+    lane = lax.broadcasted_iota(jnp.int32, (groups, 1024), 1)
+    own_group = lax.div(lane, 16) == lax.broadcasted_iota(jnp.int32, (groups, 1024), 0)
+    rates_ref[...] = jnp.dot(by_mode, own_group.astype(F32), **exact)
+    lane16 = lax.broadcasted_iota(jnp.int32, (16, 1024), 1)
+    own_mode = (lax.rem(lane16, 16) == lax.broadcasted_iota(jnp.int32, (16, 1024), 0)).astype(F32)
+    for table, ref in ((rate, lam_ref), (resid, res_ref)):
+        wide = jnp.dot(table, own_mode, **exact)
+        ref[...] = jnp.sum(jnp.where(own_group, wide, 0.0), axis=0, keepdims=True)
+    lag = lax.rem(128 + SUB - lax.broadcasted_iota(jnp.int32, (1, SUB), 1), SUB).astype(F32)
+    total = jnp.zeros((groups, SUB), F32)
+    for m in range(16):
+        total = total + resid[:, m : m + 1] * jnp.exp(-rate[:, m : m + 1] * lag)
+    taps_ref[...] = total.astype(BF16).astype(F32)
+
+
 def kernel(
-    q_hbm, k_hbm, v_hbm, w_hbm, rates_ref, lam_ref, res_ref, taps_ref, out_hbm,
+    q_hbm, k_hbm, v_hbm, w_hbm, decay_ref, resid_ref, out_hbm,
     qb, kb, vb, ub, zloc, band, bs, ent, wb, lhs, send_a, send_b, recv_b, acc, stage,
-    st_send, st_sib, st_y, st_x,
+    st_send, st_sib, st_y, st_x, rates_ref, lam_ref, res_ref, taps_ref,
     load_sem, sib_sem, st_sem, w_send, w_recv, a_sem, b_sem, fwd_sem, o_sem,
 ):
     s = lax.axis_index("seq")
@@ -72,6 +96,7 @@
     barrier = pltpu.get_barrier_semaphore()
     for dev in partners:
         pl.semaphore_signal(barrier, inc=1, device_id=dev, device_id_type=MESH)
+    tables(decay_ref, resid_ref, rates_ref, lam_ref, res_ref, taps_ref)
     pl.semaphore_wait(barrier, len(partners))
 
     own = chip(0, 0)
@@ -177,8 +202,6 @@
     st_send[0] = final.astype(BF16)
     send(st_send.at[0], st_sib, st_sem.at[0, 0], st_sem.at[1, 0], (sib, z))
 
-    weights_start()
-
     row_i = lax.broadcasted_iota(jnp.int32, (LANES, SUB), 0)
     col_i = lax.broadcasted_iota(jnp.int32, (LANES, SUB), 1)
     above = col_i - row_i > LANES
@@ -223,10 +246,8 @@
         send(st_send.at[1], st_y.at[d - 1], st_sem.at[0, d], st_sem.at[1, d], (at_xy(0, d), z))
     bs[0] = chip_total
 
+    weights_start()
     lax.fori_loop(2, 5, conv_tile, 0)
-    for r in range(2):
-        arrive(r, (1, 0))
-        arrive(r, (3, 0))
 
     row_total = decay(2048.0 * (3.0 - yf)) * bs[0]
     before = jnp.zeros((16, 1024), F32)
@@ -242,6 +263,9 @@
     bs[1] = before
 
     lax.fori_loop(5, TILES, conv_tile, 0)
+    for r in range(2):
+        arrive(r, (1, 0))
+        arrive(r, (3, 0))
 
     far = jnp.zeros((16, 1024), F32)
     for d in (1, 2, 3):
@@ -258,11 +282,13 @@
         lax.broadcasted_iota(jnp.int32, (LANES, LANES), 1), 16
     )
 
-    def gate(i, n0, n1):
+    def gate(i, half, n0, n1):
+        first_row = half * 128
+
         def gate_tile(t, carry):
             lanes = pl.ds(pl.multiple_of(t * LANES, LANES), LANES)
             lam = lam_ref[0:1, lanes]
-            step = lax.broadcasted_iota(jnp.int32, (SUB, LANES), 0).astype(F32) + 1.0
+            step = lax.broadcasted_iota(jnp.int32, (128, LANES), 0).astype(F32) + (first_row + 1.0)
             read = res_ref[0:1, lanes] * jnp.exp(-lam * step)
             read_hi = read.astype(BF16)
             read_lo = (read - read_hi.astype(F32)).astype(BF16)
@@ -280,111 +306,126 @@
                 jnp.concatenate([hi, lo, hi], axis=0),
                 preferred_element_type=F32,
             )
-            for k, (n, dst) in enumerate(((n0, send_a.at[i]), (n1, lhs.at[i, par]))):
-                rows = pl.ds(pl.multiple_of(n * 256, 256), 256)
+            for k, (n, dst) in enumerate(((n0, send_a.at[i, half]), (n1, lhs.at[i, half, par]))):
+                rows = pl.ds(pl.multiple_of(n * 256 + first_row, 128), 128)
                 zz = zloc[rows, lanes] + carried[:, k * LANES : (k + 1) * LANES]
-                dst[pl.ds(0, 256), lanes] = (qb[rows, lanes].astype(F32) * zz).astype(BF16)
+                dst[pl.ds(0, 128), lanes] = (qb[rows, lanes].astype(F32) * zz).astype(BF16)
             return carry
 
         lax.fori_loop(0, TILES, gate_tile, 0)
-        send(send_a.at[i], lhs.at[i, par, pl.ds(0, 256)], a_sem.at[0, i], a_sem.at[1, i], (s, z_a))
         send(
-            lhs.at[i, par, pl.ds(0, 256)], lhs.at[i, par, pl.ds(256, 256)],
-            fwd_sem.at[0, i, 0], fwd_sem.at[1, i, 0], (sib, z),
-        )
-
-    gate(0, 3 - z_a, 3 - z)
-    gate(1, z_a, z)
-
+            send_a.at[i, half], lhs.at[i, half, par, pl.ds(0, 128)],
+            a_sem.at[0, i, half], a_sem.at[1, i, half], (s, z_a),
+        )
+        send(
+            lhs.at[i, half, par, pl.ds(0, 128)], lhs.at[i, half, par, pl.ds(128, 128)],
+            fwd_sem.at[0, i, half, 0], fwd_sem.at[1, i, half, 0], (sib, z),
+        )
+
+    gate(0, 0, 3 - z_a, 3 - z)
+    gate(0, 1, 3 - z_a, 3 - z)
+    for r in range(2):
+        arrive(r, (0, 1))
+        arrive(r, (0, 3))
+    gate(1, 0, z_a, z)
+    gate(1, 1, z_a, z)
     for r in range(2):
         arrive(r, (2, 0))
 
-    def gathered(i):
-        ref = lhs.at[i, 1 - par, pl.ds(0, 256)]
-        remote(ref, ref, a_sem.at[0, i], a_sem.at[1, i], (s, z_a)).wait_recv()
+    def gathered(i, half):
+        ref = lhs.at[i, half, 1 - par, pl.ds(0, 128)]
+        remote(ref, ref, a_sem.at[0, i, half], a_sem.at[1, i, half], (s, z_a)).wait_recv()
         send(
-            ref, lhs.at[i, 1 - par, pl.ds(256, 256)],
-            fwd_sem.at[0, i, 1], fwd_sem.at[1, i, 1], (sib, z),
-        )
-
-    def gathered_sib(i):
+            ref, lhs.at[i, half, 1 - par, pl.ds(128, 128)],
+            fwd_sem.at[0, i, half, 1], fwd_sem.at[1, i, half, 1], (sib, z),
+        )
+
+    def gathered_sib(i, half):
         for f, h in ((0, par), (1, 1 - par)):
-            ref = lhs.at[i, h, pl.ds(256, 256)]
-            remote(ref, ref, fwd_sem.at[0, i, f], fwd_sem.at[1, i, f], (sib, z)).wait_recv()
-
-    def multiply(i, j):
-        def half(m, carry):
-            rows = pl.ds(pl.multiple_of(m * 256, 256), 256)
-            left = jnp.concatenate([lhs[i, 0, rows, :], lhs[i, 1, rows, :]], axis=1)
-            right = jnp.concatenate(
-                [
-                    jnp.concatenate([wb[chip(*rel), r, h] for rel in ORDER[2 * j : 2 * j + 2]], axis=1)
-                    for h in range(2)
-                    for r in range(2)
-                ],
-                axis=0,
-            )
-            val = jnp.dot(left, right, preferred_element_type=F32)
-            if i == 0:
-                send_b[j, rows, :] = val.astype(BF16)
-            else:
-                acc[j, rows, :] = val
-            return carry
-
-        lax.fori_loop(0, 2, half, 0)
+            ref = lhs.at[i, half, h, pl.ds(128, 128)]
+            remote(ref, ref, fwd_sem.at[0, i, half, f], fwd_sem.at[1, i, half, f], (sib, z)).wait_recv()
+
+    def multiply(i, half, j):
+        left = jnp.concatenate([lhs[i, half, 0], lhs[i, half, 1]], axis=1)
+        right = jnp.concatenate(
+            [
+                jnp.concatenate([wb[chip(*rel), r, h] for rel in ORDER[2 * j : 2 * j + 2]], axis=1)
+                for h in range(2)
+                for r in range(2)
+            ],
+            axis=0,
+        )
+        return jnp.dot(left, right, preferred_element_type=F32)
 
     def need(j):
         for dx, dy in ORDER[2 * j : 2 * j + 2]:
             arrive(0, (dx, dy))
             arrive(1, (dy, dx))
 
-    def partial(j):
+    def partial(j, half):
         need(j)
-        multiply(0, j)
-        send(send_b.at[j], recv_b.at[j], b_sem.at[0, j], b_sem.at[1, j], (s, z_b))
+        send_b[j, half] = multiply(0, half, j).astype(BF16)
+        send(send_b.at[j, half], recv_b.at[j, half], b_sem.at[0, j, half], b_sem.at[1, j, half], (s, z_b))
+
+    def keep(j, half):
+        acc[j, half] = multiply(1, half, j)
 
     outs = []
 
-    def finish(j):
-        remote(recv_b.at[j], recv_b.at[j], b_sem.at[0, j], b_sem.at[1, j], (s, z_b)).wait_recv()
-        val = (acc[j] + recv_b[j].astype(F32)).astype(BF16)
+    def finish(j, half):
+        ref = recv_b.at[j, half]
+        remote(ref, ref, b_sem.at[0, j, half], b_sem.at[1, j, half], (s, z_b)).wait_recv()
+        val = (acc[j, half] + recv_b[j, half].astype(F32)).astype(BF16)
         for k in range(2):
             cols = pl.ds(pl.multiple_of(chip(*ORDER[2 * j + k]) * 256 + c * 128, 128), 128)
             part = val[:, k * LANES : (k + 1) * LANES]
-            stage[j, k, 0] = part[:256]
-            stage[j, k, 1] = part[256:]
-            cp = pltpu.make_async_copy(stage.at[j, k, 0], out_hbm.at[:, cols], o_sem.at[0, 2 * j + k])
+            stage[j, half, k, 0] = part[:128]
+            stage[j, half, k, 1] = part[128:]
+            place = out_hbm.at[pl.ds(half * 128, 128), cols]
+            cp = pltpu.make_async_copy(stage.at[j, half, k, 0], place, o_sem.at[0, 2 * j + k, half])
             cp.start()
             outs.append(cp)
             send(
-                stage.at[j, k, 1], out_hbm.at[:, cols],
-                o_sem.at[1, 2 * j + k], o_sem.at[2, 2 * j + k], (sib, z),
+                stage.at[j, half, k, 1], place,
+                o_sem.at[1, 2 * j + k, half], o_sem.at[2, 2 * j + k, half], (sib, z),
             )
 
-    gathered(0)
-    gathered_sib(0)
-    partial(0)
-    partial(1)
-    partial(2)
-    gathered(1)
-    gathered_sib(1)
-    multiply(1, 0)
-    for j in range(3, CHUNKS):
-        partial(j)
-        multiply(1, j - 2)
-        finish(j - 3)
-    multiply(1, CHUNKS - 2)
-    multiply(1, CHUNKS - 1)
-    for j in range(CHUNKS - 3, CHUNKS):
-        finish(j)
+    gathered(0, 0)
+    gathered_sib(0, 0)
+    partial(0, 0)
+    partial(1, 0)
+    gathered(0, 1)
+    gathered_sib(0, 1)
+    partial(0, 1)
+    partial(1, 1)
+    gathered(1, 0)
+    partial(2, 0)
+    partial(2, 1)
+    gathered(1, 1)
+    partial(3, 0)
+    partial(3, 1)
+    gathered_sib(1, 0)
+    gathered_sib(1, 1)
+    for j in range(4, CHUNKS):
+        for half in range(2):
+            partial(j, half)
+            keep(j - 4, half)
+            finish(j - 4, half)
+    for j in range(CHUNKS - 4, CHUNKS):
+        for half in range(2):
+            keep(j, half)
+    for j in range(CHUNKS - 4, CHUNKS):
+        for half in range(2):
+            finish(j, half)
 
     for j in range(CHUNKS):
-        for k in range(2):
-            cols = pl.ds(pl.multiple_of(chip(*ORDER[2 * j + k]) * 256 + (1 - c) * 128, 128), 128)
-            remote(
-                stage.at[j, k, 1], out_hbm.at[:, cols],
-                o_sem.at[1, 2 * j + k], o_sem.at[2, 2 * j + k], (sib, z),
-            ).wait_recv()
+        for half in range(2):
+            for k in range(2):
+                cols = pl.ds(pl.multiple_of(chip(*ORDER[2 * j + k]) * 256 + (1 - c) * 128, 128), 128)
+                remote(
+                    stage.at[j, half, k, 1], out_hbm.at[pl.ds(half * 128, 128), cols],
+                    o_sem.at[1, 2 * j + k, half], o_sem.at[2, 2 * j + k, half], (sib, z),
+                ).wait_recv()
     for cp in outs:
         cp.wait()
     for cp in pending:
@@ -392,20 +433,13 @@
 
 
 def on_device(query_feat, key_feat, value_feat, decay_rates, residues, out_weight):
-    groups = decay_rates.shape[0]
-    lag = jnp.mod(128 - jnp.arange(SUB), SUB).astype(F32)
-    taps = jnp.sum(residues[:, :, None] * jnp.exp(-decay_rates[:, :, None] * lag), axis=1)
-    taps = taps.astype(BF16).astype(F32)
-    rates = jnp.repeat(decay_rates.T, 16, axis=1)
-    lam = decay_rates.reshape(1, -1)
-    res = residues.reshape(1, -1)
     n_w = 2 + 2 * (2 + 2) * 5
     hbm = pl.BlockSpec(memory_space=pl.ANY)
     vmem = pl.BlockSpec(memory_space=pltpu.VMEM)
     return pl.pallas_call(
         kernel,
         out_shape=jax.ShapeDtypeStruct((256, 4096), BF16),
-        in_specs=[hbm] * 4 + [vmem] * 4,
+        in_specs=[hbm] * 4 + [vmem] * 2,
         out_specs=hbm,
         scratch_shapes=[
             pltpu.VMEM((1024, 1024), BF16),
@@ -417,30 +451,34 @@
             pltpu.VMEM((4, 16, 1024), F32),
             pltpu.VMEM((4, 16, 1024), F32),
             pltpu.VMEM((CHIPS, 2, 2, 512, 128), BF16),
-            pltpu.VMEM((2, 2, 512, 1024), BF16),
-            pltpu.VMEM((2, 256, 1024), BF16),
-            pltpu.VMEM((CHUNKS, 512, 256), BF16),
-            pltpu.VMEM((CHUNKS, 512, 256), BF16),
-            pltpu.VMEM((CHUNKS, 512, 256), F32),
-            pltpu.VMEM((CHUNKS, 2, 2, 256, 128), BF16),
+            pltpu.VMEM((2, 2, 2, 256, 1024), BF16),
+            pltpu.VMEM((2, 2, 128, 1024), BF16),
+            pltpu.VMEM((CHUNKS, 2, 256, 256), BF16),
+            pltpu.VMEM((CHUNKS, 2, 256, 256), BF16),
+            pltpu.VMEM((CHUNKS, 2, 256, 256), F32),
+            pltpu.VMEM((CHUNKS, 2, 2, 2, 128, 128), BF16),
             pltpu.VMEM((3, 16, 1024), BF16),
             pltpu.VMEM((16, 1024), BF16),
             pltpu.VMEM((3, 16, 1024), BF16),
             pltpu.VMEM((3, 16, 1024), BF16),
+            pltpu.VMEM((16, 1024), F32),
+            pltpu.VMEM((1, 1024), F32),
+            pltpu.VMEM((1, 1024), F32),
+            pltpu.VMEM((64, 256), F32),
             pltpu.SemaphoreType.DMA((5,)),
             pltpu.SemaphoreType.DMA((1,)),
             pltpu.SemaphoreType.DMA((2, 7)),
             pltpu.SemaphoreType.DMA((n_w,)),
             pltpu.SemaphoreType.DMA((n_w,)),
-            pltpu.SemaphoreType.DMA((2, 2)),
-            pltpu.SemaphoreType.DMA((2, CHUNKS)),
             pltpu.SemaphoreType.DMA((2, 2, 2)),
-            pltpu.SemaphoreType.DMA((3, 2 * CHUNKS)),
+            pltpu.SemaphoreType.DMA((2, CHUNKS, 2)),
+            pltpu.SemaphoreType.DMA((2, 2, 2, 2)),
+            pltpu.SemaphoreType.DMA((3, 2 * CHUNKS, 2)),
         ],
         compiler_params=pltpu.CompilerParams(
             collective_id=0, has_side_effects=True, vmem_limit_bytes=60 * 1024 * 1024
         ),
-    )(query_feat, key_feat, value_feat, out_weight, rates, lam, res, taps)
+    )(query_feat, key_feat, value_feat, out_weight, decay_rates, residues)
 
 
 def solution(mesh):

time: 122 us -> 102 us (0.84)
  Pallas kernels: 112 us -> 95.6 us
  local copies, waits for them, and re-layouts: 7.92 us -> 5.9 us
  other arithmetic: 1.77 us -> 0 us
    pallas_call x1, Pallas kernels: 112 us -> 95.6 us  [on_device(): pl.pallas_call(kernel, out_shape=jax.ShapeDtypeStruct((256, 4096), BF16),...]
    reshape x3 -> x0, local copies, waits for them, and re-layouts: 2.26 us -> none  [the longest x1 0.9 us: on_device(): rates = jnp.repeat(decay_rates.T, 16, axis=1)]
where the time goes in v2:
time: 102 us
  Pallas kernels  95.6 us (94%)
  local copies, waits for them, and re-layouts  5.9 us (6%)
    pallas_call x1, Pallas kernels, on_device(): pl.pallas_call(kernel, out_shape=jax.ShapeDtypeStruct((256, 4096), BF16),...  95.6 us
    unnamed x3, local copies, waits for them, and re-layouts  5.9 us

profile of v2, /device:TPU:1, one launch (start us, length us, event | category | flops | bytes accessed | tf_op | source)
XLA Modules:
  0.0 101.5 jit_solution(1029220599590164676)
XLA Ops:
  0.0 1.4 %copy.7.decay_ref = f32[64,16]{1,0:T(8,128)} copy(f32[64,16]{0,1:T(8,128)} %param.9) | data formatting | bytes 8192 | tf_op args[3]
  1.4 1.4 %copy.8.resid_ref = f32[64,16]{1,0:T(8,128)} copy(f32[64,16]{0,1:T(8,128)} %param.10) | data formatting | bytes 8192 | tf_op args[4]
  2.8 95.6 %shard_map.64 = bf16[256,4096]{1,0:T(8,128)(2,1)} custom-call(bf16[1024,1024]{1,0:T(8,128)(2,1)} %q_hbm.1, bf16[1024,1024]{1,0:T(8,128)(2,1)} %k_hbm.1, bf16[1024,1024]{1,0:T(8,128)(2,1)} %v_hbm.1, bf16[1024,128]{1,0:T(8,128)(2,1)} %w_hbm.1, f32[64,16]{1,0:T(8,128)} %copy.7.decay_ref, f32[64,16]{1,0:T(8,128)} %copy.8.resid_ref), custom_call_target="tpu_custom_call" | custom-call | tf_op jit(solution)/shard_map/pallas_call | solution.py:439
  98.4 3.1 %copy.10 = bf16[256,4096]{1,0:T(8,128)(2,1)} copy(bf16[256,4096]{1,0:T(8,128)(2,1)} %shard_map.64) | data formatting | bytes 4194304
